TPU v7x, 256 devices: a whole 4x4x8 slice. The times are simulated.
256 devices in a mesh: leaf: 4 (over y), row: 16 (over z, core), col: 4 (over x).
Axes of the slice: x: 4, y: 4, z: 8, core: 2. Of those that a mesh axis runs over, the one named last changes fastest.
Arguments:
- anc_inverse: float32 [24, 24, 512, 512], P('leaf', None, 'row', 'col'), may hold values from -6 to 6, as said below
- struct_one: int32 [12, 5], P('leaf'), may hold values from 0 to 23, as said below
- lower_one: float32 [12, 5, 512, 512], P('leaf', None, 'row', 'col'), may hold values from -0.125 to 0.125
- pivot_inv_one: float32 [12, 512, 512], P('leaf', 'row', 'col'), may hold values from -6 to 6, as said below
- lower_two: float32 [24, 6, 512, 512], P('leaf', None, 'row', 'col'), may hold values from -0.109375 to 0.109375
- pivot_inv_two: float32 [24, 512, 512], P('leaf', 'row', 'col'), may hold values from -6 to 6, as said below
Outputs:
- offdiag_one: float32 [12, 5, 512, 512], P('leaf', None, 'row', 'col')
- diag_one: float32 [12, 512, 512], P('leaf', 'row', 'col')
- offdiag_two: float32 [24, 6, 512, 512], P('leaf', None, 'row', 'col')
- diag_two: float32 [24, 512, 512], P('leaf', 'row', 'col')
Inputs may be any that keep to these rules, and one draw needn't show every extreme that they name: `struct_one`: each row lists 5 different separator block numbers in increasing order. symmetric: anc_inverse[b, a] is the transpose of anc_inverse[a, b]. `pivot_inv_one`: every block equals its transpose. `pivot_inv_two`: every block equals its transpose.
All inputs are finite; a program needn't handle non-finite values.
Results may differ from a plain program's by a relative error of at most 0.0001.
Values sent between devices are 32-bit elements; how exact they have to be, the bound alone decides.
A program may use at most 64 MiB of HBM per device.

v0:
```python
import jax
import jax.numpy as jnp
from jax import lax
from jax.sharding import PartitionSpec as P

highest = lax.Precision.HIGHEST


def on_device(anc_inverse, struct_one, lower_one, pivot_inv_one, lower_two, pivot_inv_two):
    level_nodes, struct_len = struct_one.shape
    tile_rows = lower_one.shape[2]
    tile_cols = lower_one.shape[3]
    children = lower_two.shape[0] // level_nodes
    one_rows = lax.all_gather(lower_one, "row", axis=2, tiled=True)
    one_cols, two_cols = (
        lax.all_gather(lower_one, "col", axis=3, tiled=True),
        lax.all_gather(lower_two, "col", axis=3, tiled=True),
    )
    ancestors = lax.all_gather(anc_inverse, "leaf", axis=0, tiled=True)
    selected = ancestors[struct_one[:, :, None], struct_one[:, None, :]]
    stripes = lax.all_gather(selected, "col", axis=4, tiled=True)
    offdiag_one = -jnp.einsum("mstik,mtkj->msij", stripes, one_rows, precision=highest)
    cols_piece = one_cols
    summed_one = lax.psum_scatter(
        jnp.einsum("mski,mskj->imj", cols_piece, offdiag_one, precision=highest),
        "row",
        scatter_dimension=0,
        tiled=True,
    )
    diag_one = pivot_inv_one - jnp.transpose(summed_one, (1, 0, 2))
    parent_col = jnp.concatenate([offdiag_one, diag_one[:, None]], axis=1)
    parent_stripe = lax.all_gather(parent_col, "col", axis=3, tiled=True)
    two_rows = lax.all_gather(lower_two, "row", axis=2, tiled=True)
    rows_split = two_rows.reshape(
        level_nodes, children, struct_len + 1, two_rows.shape[2], tile_cols
    )
    cols_split = two_cols.reshape(
        level_nodes, children, struct_len + 1, tile_rows, two_cols.shape[3]
    )
    local_split = lower_two.reshape(level_nodes, children, struct_len + 1, tile_rows, tile_cols)
    upper_part = jnp.einsum(
        "mstik,mctkj->mcsij", stripes, rows_split[:, :, :struct_len], precision=highest
    )
    upper_part = upper_part + jnp.einsum(
        "msik,mckj->mcsij",
        parent_stripe[:, :struct_len],
        rows_split[:, :, struct_len],
        precision=highest,
    )
    stripe_piece = parent_stripe[:, :struct_len]
    summed_parent = lax.psum_scatter(
        jnp.einsum(
            "mqki,mcqkj->imcj", stripe_piece, local_split[:, :, :struct_len], precision=highest
        ),
        "row",
        scatter_dimension=0,
        tiled=True,
    )
    parent_row = jnp.transpose(summed_parent, (1, 2, 0, 3))
    parent_row = parent_row + jnp.einsum(
        "mik,mckj->mcij",
        parent_stripe[:, struct_len],
        rows_split[:, :, struct_len],
        precision=highest,
    )
    offdiag_split = -jnp.concatenate([upper_part, parent_row[:, :, None]], axis=2)
    cols_piece = cols_split
    summed_two = lax.psum_scatter(
        jnp.einsum("mcpki,mcpkj->imcj", cols_piece, offdiag_split, precision=highest),
        "row",
        scatter_dimension=0,
        tiled=True,
    )
    diag_two = pivot_inv_two - jnp.transpose(summed_two, (1, 2, 0, 3)).reshape(
        level_nodes * children, tile_rows, tile_cols
    )
    offdiag_two = offdiag_split.reshape(
        level_nodes * children, struct_len + 1, tile_rows, tile_cols
    )
    return (offdiag_one, diag_one, offdiag_two, diag_two)


def solution(mesh):
    placed = (
        P("leaf", None, "row", "col"),
        P("leaf", None),
        P("leaf", None, "row", "col"),
        P("leaf", "row", "col"),
        P("leaf", None, "row", "col"),
        P("leaf", "row", "col"),
    )
    return jax.shard_map(
        on_device,
        mesh=mesh,
        in_specs=placed,
        out_specs=(
            P("leaf", None, "row", "col"),
            P("leaf", "row", "col"),
            P("leaf", None, "row", "col"),
            P("leaf", "row", "col"),
        ),
        check_vma=False,
    )
```

profile of v0, /device:TPU:1, one launch (start us, length us, event | category | flops | bytes accessed | tf_op | source)
XLA Modules:
  0.0 604.5 jit_solution(8348671050504362168)
XLA Ops:
  8.0 0.7 all-gather.11.cloned.1.call-update
  8.9 99.3 %all-gather.7.cloned.1.call-done = f32[24,24,32,128]{3,2,1,0:T(8,128)} async-done(((f32[6,24,32,128]{3,2,1,0:T(8,128)}), f32[24,24,32,128]{3,2,1,0:T(8,128)}) %all-gather.7.cloned.1.call-update) | async-done | bytes 9437200 | tf_op jit(solution)/shard_map/all_gather | solution.py:19
  108.2 5.9 gather_fusion
  114.2 13.2 %all_gather.24 = f32[3,5,32,512]{3,2,1,0:T(8,128)S(1)} all-gather(f32[3,5,32,128]{3,2,1,0:T(8,128)S(1)} %copy-done.3), channel_id=1, replica_groups=mesh['leaf'=4,'row'=16,'col'=4] {'col'}, dimensions={3}, use_global_device_ids=true | all-gather | bytes 1228800 | tf_op jit(solution)/shard_map/all_gather | solution.py:16
  127.4 26.1 %all-gather.11.cloned.1.call-done = f32[3,5,512,128]{3,2,1,0:T(8,128)} async-done(((f32[3,5,32,128]{3,2,1,0:T(8,128)}), f32[3,5,512,128]{3,2,1,0:T(8,128)}) %all-gather.11.cloned.1.call-update) | async-done | bytes 3932176 | tf_op jit(solution)/shard_map/all_gather | solution.py:14
  153.5 59.6 %all-gather.9.cloned.1.call-done = f32[3,5,5,32,512]{4,3,2,1,0:T(8,128)} async-done(((f32[3,5,5,32,128]{4,3,2,1,0:T(8,128)}), f32[3,5,5,32,512]{4,3,2,1,0:T(8,128)}) %all-gather.9.cloned.1.call-update) | async-done | bytes 4915216 | tf_op jit(solution)/shard_map/all_gather | solution.py:21
  213.1 8.0 %fusion.22 = f32[3,5,32,128]{3,2,1,0:T(8,128)S(1)} fusion(f32[3,5,5,32,512]{4,3,2,1,0:T(8,128)} %all-gather.9.cloned.1.call-done, f32[3,5,512,128]{3,2,1,0:T(8,128)} %all-gather.11.cloned.1.call-done), kind=kOutput, calls=%fused_computation.19 | convolution fusion | flops 1887498240 | bytes 9093120 | tf_op jit(solution)/shard_map/mstik,mtkj->msij/dot_general | solution.py:22
  221.1 3.6 convolution_bitcast_fusion.2
  224.8 55.9 %reduce-scatter.3.cloned.1.call-done = f32[32,3,128]{2,0,1:T(8,128)} async-done(((f32[512,3,128]{2,0,1:T(8,128)}), f32[32,3,128]{2,0,1:T(8,128)}) %reduce-scatter.3.cloned.1.call-update) | async-done | bytes 49168 | tf_op jit(solution)/shard_map/reduce_scatter | solution.py:24
  280.7 0.8 bitcast_subtract_fusion.1
  281.5 0.7 pad_maximum_fusion
  282.9 30.0 %all-gather.15.cloned.1.call-done = f32[3,6,32,512]{3,2,1,0:T(8,128)} async-done(((f32[3,6,32,128]{3,2,1,0:T(8,128)}), f32[3,6,32,512]{3,2,1,0:T(8,128)}) %all-gather.15.cloned.1.call-update) | async-done | bytes 1179664 | tf_op jit(solution)/shard_map/all_gather | solution.py:32
  312.9 5.1 convolution_bitcast_fusion.1
  319.0 59.0 %all-gather.13.cloned.1.call-done = f32[6,6,512,128]{3,2,1,0:T(8,128)} async-done(((f32[6,6,32,128]{3,2,1,0:T(8,128)}), f32[6,6,512,128]{3,2,1,0:T(8,128)}) %all-gather.13.cloned.1.call-update) | async-done | bytes 9437200 | tf_op jit(solution)/shard_map/all_gather | solution.py:33
  378.0 10.1 %fusion.10 = f32[3,5,32,2,128]{4,2,3,1,0:T(8,128)S(1)} fusion(f32[3,2,6,512,128]{4,3,2,1,0:T(8,128)} %bitcast.107, f32[3,5,5,32,512]{4,3,2,1,0:T(8,128)} %all-gather.9.cloned.1.call-done), kind=kOutput, calls=%fused_computation.15 | convolution fusion | flops 3774873600 | bytes 13271040 | tf_op jit(solution)/shard_map/mstik,mctkj->mcsij/dot_general | solution.py:41
  388.0 2.6 fusion.16
  390.7 43.4 %reduce-scatter.5.cloned.1.call-done = f32[32,3,2,128]{3,0,2,1:T(8,128)} async-done(((f32[512,3,2,128]{3,0,2,1:T(8,128)}), f32[32,3,2,128]{3,0,2,1:T(8,128)}) %reduce-scatter.5.cloned.1.call-update) | async-done | bytes 98320 | tf_op jit(solution)/shard_map/reduce_scatter | solution.py:51
  434.1 2.4 fusion.28
  436.5 39.2 %all-gather.17.cloned.1.call-done = f32[6,6,32,512]{3,2,1,0:T(8,128)} async-done(((f32[6,6,32,128]{3,2,1,0:T(8,128)}), f32[6,6,32,512]{3,2,1,0:T(8,128)}) %all-gather.17.cloned.1.call-update) | async-done | bytes 2359312 | tf_op jit(solution)/shard_map/all_gather | solution.py:17
  475.7 3.4 convolution_bitcast_fusion
  479.1 2.1 copy.29
  482.5 0.9 maximum_negate_fusion
  483.4 112.9 %all-reduce.3.cloned.1.call-done = f32[512,3,2,128]{3,2,1,0:T(2,128)} async-done(((f32[512,3,2,128]{3,2,1,0:T(2,128)}), f32[512,3,2,128]{3,2,1,0:T(2,128)}) %all-reduce.3.cloned.1.call-update) | async-done | bytes 1572880
  596.3 0.9 constant_dynamic-slice_fusion
  (42 shorter events, 4.0 us)
Async XLA Ops:
  7.2 1.6 copy-start.7
  7.2 101.0 %all-gather.7.cloned.1.call-start = ((), (), s32[]{:S(2)}) async-start(), calls=%async_computation.2 | async-start | bytes 11796480 | tf_op jit(solution)/shard_map/all_gather | solution.py:19
  7.9 106.3 %copy-start.3 = (f32[3,5,32,128]{3,2,1,0:T(8,128)S(1)}, f32[3,5,32,128]{3,2,1,0:T(8,128)}, u32[]{:S(2)}) copy-start(f32[3,5,32,128]{3,2,1,0:T(8,128)} %param.8) | copy-start | bytes 737284
  7.9 145.6 %all-gather.11.cloned.1.call-start = ((), (), s32[]{:S(2)}) async-start(), calls=%async_computation.4 | async-start | bytes 4177920 | tf_op jit(solution)/shard_map/all_gather | solution.py:14
  8.7 204.4 %all-gather.9.cloned.1.call-start = ((), (), s32[]{:S(2)}) async-start(), calls=%async_computation.3 | async-start | bytes 6144000 | tf_op jit(solution)/shard_map/all_gather | solution.py:21
  114.1 166.6 %reduce-scatter.3.cloned.1.call-start = ((), (), s32[]{:S(2)}) async-start(), calls=%async_computation.5 | async-start | bytes 835584 | tf_op jit(solution)/shard_map/reduce_scatter | solution.py:24
  221.1 96.9 %copy-start.2 = (f32[3,5,32,128]{3,2,1,0:T(8,128)}, f32[3,5,32,128]{3,2,1,0:T(8,128)S(1)}, u32[]{:S(2)}) copy-start(f32[3,5,32,128]{3,2,1,0:T(8,128)S(1)} %fusion.22) | copy-start | bytes 737284
  221.1 59.6 %copy-start.6 = (f32[3,32,128]{2,1,0:T(8,128)S(1)}, f32[3,32,128]{2,1,0:T(8,128)}, u32[]{:S(2)}) copy-start(f32[3,32,128]{2,1,0:T(8,128)} %param.9) | copy-start | bytes 147460
  221.1 91.8 %copy-start = (f32[6,6,32,128]{3,2,1,0:T(8,128)S(1)}, f32[6,6,32,128]{3,2,1,0:T(8,128)}, u32[]{:S(2)}) copy-start(f32[6,6,32,128]{3,2,1,0:T(8,128)} %param.10) | copy-start | bytes 1769476
  224.7 88.2 %all-gather.15.cloned.1.call-start = ((), (), s32[]{:S(2)}) async-start(), calls=%async_computation.7 | async-start | bytes 1474560 | tf_op jit(solution)/shard_map/all_gather | solution.py:32
  281.5 36.4 %copy-start.4 = (f32[3,32,128]{2,1,0:T(8,128)}, f32[3,32,128]{2,1,0:T(8,128)S(1)}, u32[]{:S(2)}) copy-start(f32[3,32,128]{2,1,0:T(8,128)S(1)} %bitcast_subtract_fusion.1) | copy-start | bytes 147460
  282.3 95.6 %all-gather.13.cloned.1.call-start = ((), (), s32[]{:S(2)}) async-start(), calls=%async_computation.6 | async-start | bytes 10027008 | tf_op jit(solution)/shard_map/all_gather | solution.py:33
  282.9 151.2 %reduce-scatter.5.cloned.1.call-start = ((), (), s32[]{:S(2)}) async-start(), calls=%async_computation.8 | async-start | bytes 1671168 | tf_op jit(solution)/shard_map/reduce_scatter | solution.py:51
  318.0 157.7 %all-gather.17.cloned.1.call-start = ((), (), s32[]{:S(2)}) async-start(), calls=%async_computation.9 | async-start | bytes 2949120 | tf_op jit(solution)/shard_map/all_gather | solution.py:17
  318.8 277.6 %all-reduce.3.cloned.1.call-start = ((), (), s32[]{:S(2)}) async-start(), calls=%async_computation.10 | async-start | bytes 3145728
  377.9 10.1 %copy-start.1 = (f32[3,6,32,512]{3,2,1,0:T(8,128)S(1)}, f32[3,6,32,512]{3,2,1,0:T(8,128)}, u32[]{:S(2)}) copy-start(f32[3,6,32,512]{3,2,1,0:T(8,128)} %all-gather.15.cloned.1.call-done) | copy-start | bytes 3538948
  479.0 2.2 copy-start.8
  481.2 116.0 %copy-start.5 = (f32[6,32,128]{2,1,0:T(8,128)S(1)}, f32[6,32,128]{2,1,0:T(8,128)}, u32[]{:S(2)}) copy-start(f32[6,32,128]{2,1,0:T(8,128)} %param.11) | copy-start | bytes 294916
Sparse Core Ops, SparseCore 0:
  9.8 98.3 all-gather.6
  110.0 43.3 all-gather.10
  155.3 57.7 all-gather.8
  224.9 55.8 reduce-scatter.2
  283.1 29.7 all-gather.14
  314.8 63.1 all-gather.12
  380.6 53.3 reduce-scatter.4
  435.9 39.7 all-gather.16
  481.4 114.9 all-reduce.2
where the time goes:
time: 605 us; the launch traced here: 604 us
  waiting for transfers between devices  528 us (87%)
  matrix products  35.1 us (6%)
  between operations  14.7 us (2%)
  blocking collectives  13.2 us (2%)
  local copies, waits for them, and re-layouts  9.73 us (2%)
    unnamed x10, waiting for transfers between devices  116 us
    all_gather x1, waiting for transfers between devices, on_device(): ancestors = lax.all_gather(anc_inverse, 'leaf', axis=0, tiled=True)  99.3 us
    all_gather x1, waiting for transfers between devices, on_device(): stripes = lax.all_gather(selected, 'col', axis=4, tiled=True)  59.6 us
    all_gather x1, waiting for transfers between devices, on_device(): two_rows = lax.all_gather(lower_two, 'row', axis=2, tiled=True)  59 us
    reduce_scatter x1, waiting for transfers between devices, on_device(): lax.psum_scatter(jnp.einsum('mski,mskj->imj', cols_piece, offdiag_one, pr...  55.9 us
    reduce_scatter x1, waiting for transfers between devices, on_device(): lax.psum_scatter(jnp.einsum('mqki,mcqkj->imcj', stripe_piece, local_split...  43.4 us
    all_gather x1, waiting for transfers between devices, on_device(): lax.all_gather(lower_two, 'col', axis=3, tiled=True)  39.2 us
    all_gather x1, waiting for transfers between devices, on_device(): parent_stripe = lax.all_gather(parent_col, 'col', axis=3, tiled=True)  30 us
  transfers between devices with their start and end apart: 9, of which 9 were waited for; matrix products, arithmetic and copies ran while one was open for 5% of the time, Pallas kernels for 0%

commit v1 on v0

--- a/solution.py
+++ b/solution.py
@@ -16,7 +16,23 @@
         lax.all_gather(lower_one, "col", axis=3, tiled=True),
         lax.all_gather(lower_two, "col", axis=3, tiled=True),
     )
-    ancestors = lax.all_gather(anc_inverse, "leaf", axis=0, tiled=True)
+    ways, here, step = (lax.axis_size("leaf"), lax.axis_index("leaf"), anc_inverse.shape[0])
+    dims = [n * ways if d == 0 else n for d, n in enumerate(anc_inverse.shape)]
+    full = lax.dynamic_update_slice_in_dim(
+        jnp.zeros(dims, anc_inverse.dtype), anc_inverse, here * step, axis=0
+    )
+    going_up = going_down = anc_inverse
+    for far in range(1, ways // 2 + 1):
+        going_up = lax.ppermute(going_up, "leaf", [(d, (d + 1) % ways) for d in range(ways)])
+        full = lax.dynamic_update_slice_in_dim(full, going_up, (here - far) % ways * step, axis=0)
+        if 2 * far < ways:
+            going_down = lax.ppermute(
+                going_down, "leaf", [(d, (d - 1) % ways) for d in range(ways)]
+            )
+            full = lax.dynamic_update_slice_in_dim(
+                full, going_down, (here + far) % ways * step, axis=0
+            )
+    ancestors = full
     selected = ancestors[struct_one[:, :, None], struct_one[:, None, :]]
     stripes = lax.all_gather(selected, "col", axis=4, tiled=True)
     offdiag_one = -jnp.einsum("mstik,mtkj->msij", stripes, one_rows, precision=highest)

time: 605 us -> 579 us (0.957)
  waiting for transfers between devices: 528 us -> 479 us
  local copies, waits for them, and re-layouts: 9.73 us -> 25.1 us
    all_gather x1 -> x0, waiting for transfers between devices: 99.3 us -> none  [on_device(): ancestors = lax.all_gather(anc_inverse, 'leaf', axis=0, tiled=True)]
    ppermute x0 -> x3, waiting for transfers between devices: none -> 86.6 us  [the longest x2 86.6 us: on_device(): lax.ppermute(going_up, 'leaf', [(d, (d + 1) % ways) for d in range(ways)])]
    all_gather x1, waiting for transfers between devices: 26.1 us -> 0.01 us  [on_device(): one_rows = lax.all_gather(lower_one, 'row', axis=2, tiled=True)]
    dynamic_update_slice x0 -> x4, local copies, waits for them, and re-layouts: none -> 10.5 us  [the longest x2 5.19 us: on_device(): lax.dynamic_update_slice_in_dim(full, going_up, (here - far) % ways * ste...]
    all_gather x1, waiting for transfers between devices: 59.6 us -> 50 us  [on_device(): stripes = lax.all_gather(selected, 'col', axis=4, tiled=True)]
    unnamed x10 -> x9, waiting for transfers between devices: 116 us -> 115 us
  transfers between devices with their start and end apart: 9 -> 11, of which waited for: 9 -> 9; matrix products, arithmetic and copies ran while one was open for 5% -> 8% of each run, Pallas kernels for 0% -> 0%
where the time goes in v1:
time: 579 us; the launch traced here: 578 us
  waiting for transfers between devices  479 us (83%)
  matrix products  35.2 us (6%)
  local copies, waits for them, and re-layouts  25.1 us (4%)
  between operations  15 us (3%)
  blocking collectives  14.4 us (2%)
  starting transfers between devices  5.93 us (1%)
    unnamed x9, waiting for transfers between devices  115 us
    ppermute x2, waiting for transfers between devices, on_device(): lax.ppermute(going_up, 'leaf', [(d, (d + 1) % ways) for d in range(ways)])  86.6 us
    all_gather x1, waiting for transfers between devices, on_device(): two_rows = lax.all_gather(lower_two, 'row', axis=2, tiled=True)  58.8 us
    reduce_scatter x1, waiting for transfers between devices, on_device(): lax.psum_scatter(jnp.einsum('mski,mskj->imj', cols_piece, offdiag_one, pr...  55.9 us
    all_gather x1, waiting for transfers between devices, on_device(): stripes = lax.all_gather(selected, 'col', axis=4, tiled=True)  50 us
    reduce_scatter x1, waiting for transfers between devices, on_device(): lax.psum_scatter(jnp.einsum('mqki,mcqkj->imcj', stripe_piece, local_split...  43.4 us
    all_gather x1, waiting for transfers between devices, on_device(): lax.all_gather(lower_two, 'col', axis=3, tiled=True)  39.2 us
    all_gather x1, waiting for transfers between devices, on_device(): parent_stripe = lax.all_gather(parent_col, 'col', axis=3, tiled=True)  30 us
  transfers between devices with their start and end apart: 11, of which 9 were waited for; matrix products, arithmetic and copies ran while one was open for 8% of the time, Pallas kernels for 0%

profile of v1, /device:TPU:1, one launch (start us, length us, event | category | flops | bytes accessed | tf_op | source)
XLA Modules:
  0.0 578.2 jit_solution(17114188690872214092)
XLA Ops:
  7.9 2.2 collective-permute-start
  11.7 49.1 %collective-permute-done = f32[6,24,32,128]{3,2,1,0:T(8,128)S(1)} collective-permute-done((f32[6,24,32,128]{3,2,1,0:T(8,128)}, f32[6,24,32,128]{3,2,1,0:T(8,128)S(1)}, u32[]{:S(2)}, u32[]{:S(2)}) %collective-permute-start) | collective-permute-done | bytes 2359328 | tf_op jit(solution)/shard_map/ppermute | solution.py:26
  63.3 4.9 broadcast_in_dim.10
  68.1 1.8 constant_dynamic-update-slice_fusion.3
  71.7 3.5 constant_dynamic-update-slice_fusion.1
  75.2 37.6 %collective-permute-done.2 = f32[6,24,32,128]{3,2,1,0:T(8,128)} collective-permute-done((f32[6,24,32,128]{3,2,1,0:T(8,128)S(1)}, f32[6,24,32,128]{3,2,1,0:T(8,128)}, u32[]{:S(2)}, u32[]{:S(2)}) %collective-permute-start.2) | collective-permute-done | bytes 2359328 | tf_op jit(solution)/shard_map/ppermute | solution.py:26
  112.7 3.5 constant_dynamic-update-slice_fusion
  116.2 5.9 %gather_fusion = f32[75,32,128]{2,1,0:T(8,128)} fusion(f32[24,24,32,128]{3,2,1,0:T(8,128)} %constant_dynamic-update-slice_fusion, s32[75]{0:T(128)S(1)} %reshape.41), kind=kCustom, calls=%fused_computation | custom fusion | bytes 2458200 | tf_op jit(solution)/shard_map/gather | solution.py:36
  122.2 14.4 %all_gather.20 = f32[3,5,32,512]{3,2,1,0:T(8,128)S(1)} all-gather(f32[3,5,32,128]{3,2,1,0:T(8,128)S(1)} %copy-done.4), channel_id=1, replica_groups=mesh['leaf'=4,'row'=16,'col'=4] {'col'}, dimensions={3}, use_global_device_ids=true | all-gather | bytes 1228800 | tf_op jit(solution)/shard_map/all_gather | solution.py:16
  136.6 50.0 %all-gather.6.cloned.1.call-done = f32[3,5,5,32,512]{4,3,2,1,0:T(8,128)} async-done(((f32[3,5,5,32,128]{4,3,2,1,0:T(8,128)}), f32[3,5,5,32,512]{4,3,2,1,0:T(8,128)}) %all-gather.6.cloned.1.call-update) | async-done | bytes 4915216 | tf_op jit(solution)/shard_map/all_gather | solution.py:37
  186.7 8.0 %fusion.22 = f32[3,5,32,128]{3,2,1,0:T(8,128)S(1)} fusion(f32[3,5,5,32,512]{4,3,2,1,0:T(8,128)} %all-gather.6.cloned.1.call-done, f32[3,5,512,128]{3,2,1,0:T(8,128)} %all-gather.8.cloned.1.call-done), kind=kOutput, calls=%fused_computation.19 | convolution fusion | flops 1887498240 | bytes 9093120 | tf_op jit(solution)/shard_map/mstik,mtkj->msij/dot_general | solution.py:38
  194.7 3.6 convolution_bitcast_fusion.2
  198.4 55.9 %reduce-scatter.3.cloned.1.call-done = f32[32,3,128]{2,0,1:T(8,128)} async-done(((f32[512,3,128]{2,0,1:T(8,128)}), f32[32,3,128]{2,0,1:T(8,128)}) %reduce-scatter.3.cloned.1.call-update) | async-done | bytes 49168 | tf_op jit(solution)/shard_map/reduce_scatter | solution.py:40
  256.5 30.0 %all-gather.12.cloned.1.call-done = f32[3,6,32,512]{3,2,1,0:T(8,128)} async-done(((f32[3,6,32,128]{3,2,1,0:T(8,128)}), f32[3,6,32,512]{3,2,1,0:T(8,128)}) %all-gather.12.cloned.1.call-update) | async-done | bytes 1179664 | tf_op jit(solution)/shard_map/all_gather | solution.py:48
  286.5 5.1 convolution_bitcast_fusion.1
  292.7 58.8 %all-gather.10.cloned.1.call-done = f32[6,6,512,128]{3,2,1,0:T(8,128)} async-done(((f32[6,6,32,128]{3,2,1,0:T(8,128)}), f32[6,6,512,128]{3,2,1,0:T(8,128)}) %all-gather.10.cloned.1.call-update) | async-done | bytes 9437200 | tf_op jit(solution)/shard_map/all_gather | solution.py:49
  351.5 2.6 fusion.4
  354.2 10.0 %fusion.16 = f32[3,2,5,32,128]{4,3,1,2,0:T(8,128)S(1)} fusion(f32[3,5,32,2,128]{4,2,3,1,0:T(8,128)S(1)} %fusion.4, f32[3,2,6,512,128]{4,3,2,1,0:T(8,128)} %bitcast.116, f32[3,5,5,32,512]{4,3,2,1,0:T(8,128)} %all-gather.6.cloned.1.call-done), kind=kOutput, calls=%fused_computation.17 | convolution fusion | flops 3774996480 | bytes 13762560 | tf_op jit(solution)/shard_map/mstik,mctkj->mcsij/dot_general | solution.py:57
  364.2 43.4 %reduce-scatter.5.cloned.1.call-done = f32[32,3,2,128]{3,0,2,1:T(8,128)} async-done(((f32[512,3,2,128]{3,0,2,1:T(8,128)}), f32[32,3,2,128]{3,0,2,1:T(8,128)}) %reduce-scatter.5.cloned.1.call-update) | async-done | bytes 98320 | tf_op jit(solution)/shard_map/reduce_scatter | solution.py:67
  407.5 2.4 fusion.28
  409.9 39.2 %all-gather.14.cloned.1.call-done = f32[6,6,32,512]{3,2,1,0:T(8,128)} async-done(((f32[6,6,32,128]{3,2,1,0:T(8,128)}), f32[6,6,32,512]{3,2,1,0:T(8,128)}) %all-gather.14.cloned.1.call-update) | async-done | bytes 2359312 | tf_op jit(solution)/shard_map/all_gather | solution.py:17
  449.1 3.4 convolution_bitcast_fusion
  452.5 2.1 copy.29
  456.9 112.9 %all-reduce.3.cloned.1.call-done = f32[512,3,2,128]{3,2,1,0:T(2,128)} async-done(((f32[512,3,2,128]{3,2,1,0:T(2,128)}), f32[512,3,2,128]{3,2,1,0:T(2,128)}) %all-reduce.3.cloned.1.call-update) | async-done | bytes 1572880
  (50 shorter events, 12.9 us)
Async XLA Ops:
  7.2 129.5 %all-gather.8.cloned.1.call-start = ((), (), s32[]{:S(2)}) async-start(), calls=%async_computation.3 | async-start | bytes 4177920 | tf_op jit(solution)/shard_map/all_gather | solution.py:14
  7.9 178.8 %all-gather.6.cloned.1.call-start = ((), (), s32[]{:S(2)}) async-start(), calls=%async_computation.2 | async-start | bytes 6144000 | tf_op jit(solution)/shard_map/all_gather | solution.py:37
  7.9 52.8 %collective-permute-start = (f32[6,24,32,128]{3,2,1,0:T(8,128)}, f32[6,24,32,128]{3,2,1,0:T(8,128)S(1)}, u32[]{:S(2)}, u32[]{:S(2)}) collective-permute-start(f32[6,24,32,128]{3,2,1,0:T(8,128)} %param.6), channel_id=1, source_target_pairs={{0,64},{64,128},{128,192},{192,0},{1,65},{65,129},{129,193},{193,1... | collective-permute-start | bytes 7077896 | tf_op jit(solution)/shard_map/ppermute | solution.py:26
  10.1 61.5 %collective-permute-start.1 = (f32[6,24,32,128]{3,2,1,0:T(8,128)}, f32[6,24,32,128]{3,2,1,0:T(8,128)}, u32[]{:S(2)}, u32[]{:S(2)}) collective-permute-start(f32[6,24,32,128]{3,2,1,0:T(8,128)} %param.6), channel_id=1, source_target_pairs={{0,192},{64,0},{128,64},{192,128},{1,193},{65,1},{129,65},{193,129... | collective-permute-start | bytes 7077896 | tf_op jit(solution)/shard_map/ppermute | solution.py:29
  60.7 52.0 %collective-permute-start.2 = (f32[6,24,32,128]{3,2,1,0:T(8,128)S(1)}, f32[6,24,32,128]{3,2,1,0:T(8,128)}, u32[]{:S(2)}, u32[]{:S(2)}) collective-permute-start(f32[6,24,32,128]{3,2,1,0:T(8,128)S(1)} %collective-permute-done), channel_id=1, source_target_pairs={{0,64},{64,128},{128,192},{192,0},{1,65},{65,129},{129,193},{193,1... | collective-permute-start | bytes 7077896 | tf_op jit(solution)/shard_map/ppermute | solution.py:26
  63.3 4.9 copy-start.2
  75.1 47.1 %copy-start.4 = (f32[3,5,32,128]{3,2,1,0:T(8,128)S(1)}, f32[3,5,32,128]{3,2,1,0:T(8,128)}, u32[]{:S(2)}) copy-start(f32[3,5,32,128]{3,2,1,0:T(8,128)} %param.8) | copy-start | bytes 737284
  122.2 132.2 %reduce-scatter.3.cloned.1.call-start = ((), (), s32[]{:S(2)}) async-start(), calls=%async_computation.4 | async-start | bytes 835584 | tf_op jit(solution)/shard_map/reduce_scatter | solution.py:40
  136.6 117.7 %copy-start.7 = (f32[3,32,128]{2,1,0:T(8,128)S(1)}, f32[3,32,128]{2,1,0:T(8,128)}, u32[]{:S(2)}) copy-start(f32[3,32,128]{2,1,0:T(8,128)} %param.9) | copy-start | bytes 147460
  194.7 97.0 %copy-start.3 = (f32[3,5,32,128]{3,2,1,0:T(8,128)}, f32[3,5,32,128]{3,2,1,0:T(8,128)S(1)}, u32[]{:S(2)}) copy-start(f32[3,5,32,128]{3,2,1,0:T(8,128)S(1)} %fusion.22) | copy-start | bytes 737284
  194.7 91.8 %copy-start = (f32[6,6,32,128]{3,2,1,0:T(8,128)S(1)}, f32[6,6,32,128]{3,2,1,0:T(8,128)}, u32[]{:S(2)}) copy-start(f32[6,6,32,128]{3,2,1,0:T(8,128)} %param.10) | copy-start | bytes 1769476
  198.3 88.2 %all-gather.12.cloned.1.call-start = ((), (), s32[]{:S(2)}) async-start(), calls=%async_computation.6 | async-start | bytes 1474560 | tf_op jit(solution)/shard_map/all_gather | solution.py:48
  255.1 99.0 %copy-start.5 = (f32[3,32,128]{2,1,0:T(8,128)}, f32[3,32,128]{2,1,0:T(8,128)S(1)}, u32[]{:S(2)}) copy-start(f32[3,32,128]{2,1,0:T(8,128)S(1)} %bitcast_subtract_fusion.1) | copy-start | bytes 147460
  255.9 95.6 %all-gather.10.cloned.1.call-start = ((), (), s32[]{:S(2)}) async-start(), calls=%async_computation.5 | async-start | bytes 10027008 | tf_op jit(solution)/shard_map/all_gather | solution.py:49
  256.5 151.0 %reduce-scatter.5.cloned.1.call-start = ((), (), s32[]{:S(2)}) async-start(), calls=%async_computation.7 | async-start | bytes 1671168 | tf_op jit(solution)/shard_map/reduce_scatter | solution.py:67
  286.5 65.0 %copy-start.1 = (f32[3,6,32,512]{3,2,1,0:T(8,128)S(1)}, f32[3,6,32,512]{3,2,1,0:T(8,128)}, u32[]{:S(2)}) copy-start(f32[3,6,32,512]{3,2,1,0:T(8,128)} %all-gather.12.cloned.1.call-done) | copy-start | bytes 3538948
  291.7 157.4 %all-gather.14.cloned.1.call-start = ((), (), s32[]{:S(2)}) async-start(), calls=%async_computation.8 | async-start | bytes 2949120 | tf_op jit(solution)/shard_map/all_gather | solution.py:17
  292.4 277.3 %all-reduce.3.cloned.1.call-start = ((), (), s32[]{:S(2)}) async-start(), calls=%async_computation.9 | async-start | bytes 3145728
  449.1 5.6 copy-start.8
  452.5 118.2 %copy-start.6 = (f32[6,32,128]{2,1,0:T(8,128)S(1)}, f32[6,32,128]{2,1,0:T(8,128)}, u32[]{:S(2)}) copy-start(f32[6,32,128]{2,1,0:T(8,128)} %param.11) | copy-start | bytes 294916
Sparse Core Ops, SparseCore 0:
  9.8 46.2 all-gather.7
  122.3 64.3 all-gather.5
  198.4 55.8 reduce-scatter.2
  256.7 29.7 all-gather.11
  288.3 63.1 all-gather.9
  354.1 53.3 reduce-scatter.4
  409.3 39.7 all-gather.13
  454.8 114.9 all-reduce.2
